TPU v7x, 32 devices: a whole 2x2x4 slice. The times are simulated.
32 devices in a mesh: rep: 8 (over z, y), shard: 4 (over x, core).
Axes of the slice: x: 2, y: 2, z: 4, core: 2. Of those that a mesh axis runs over, the one named last changes fastest.
Arguments:
- hidden_in: bfloat16 [32768, 1024], P(('rep', 'shard')), may hold values from -6 to 6
- teacher: bfloat16 [32768, 1024], P(('rep', 'shard')), may hold values from -6 to 6
- cotangent: bfloat16 [32768, 1024], P(('rep', 'shard')), may hold values from -6 to 6
- lengths: int32 [32], P(('rep', 'shard')), may hold values from 512 to 1024, as said below
- norm_attn: float32 [1024], replicated, may hold values from 0.5 to 1.5
- w_in: bfloat16 [1024, 6144], P('shard'), may hold values from -0.1875 to 0.1875
- w_small: bfloat16 [1024, 24], P('shard'), may hold values from -0.1875 to 0.1875
- conv_w: float32 [4, 5120], replicated, may hold values from -3 to 3
- a_log: float32 [8], replicated, may hold values from -6 to 0.5
- dt_bias: float32 [8], replicated, may hold values from -2 to 1
- norm_head: float32 [128], replicated, may hold values from 0.5 to 1.5
- w_out: bfloat16 [1024, 1024], P('shard'), may hold values from -0.1875 to 0.1875
- norm_mlp: float32 [1024], replicated, may hold values from 0.5 to 1.5
- w_mlp_in: bfloat16 [1024, 5632], P('shard'), may hold values from -0.1875 to 0.1875
- w_mlp_down: bfloat16 [2816, 1024], P('shard'), may hold values from -0.109375 to 0.109375
Outputs:
- layer_out: bfloat16 [32768, 1024], P(('rep', 'shard'))
- loss: float32 [], replicated
- grad_hidden: bfloat16 [32768, 1024], P(('rep', 'shard'))
- grad_norm_attn: float32 [1024], replicated
- grad_w_in: float32 [1024, 6144], P('shard')
- grad_w_small: float32 [1024, 24], P('shard')
- grad_conv_w: float32 [4, 5120], replicated
- grad_a_log: float32 [8], replicated
- grad_dt_bias: float32 [8], replicated
- grad_norm_head: float32 [128], replicated
- grad_w_out: float32 [1024, 1024], P('shard')
- grad_norm_mlp: float32 [1024], replicated
- grad_w_mlp_in: float32 [1024, 5632], P('shard')
- grad_w_mlp_down: float32 [2816, 1024], P('shard')
Inputs may be any that keep to these rules, and one draw needn't show every extreme that they name: `lengths`: each sequence's valid slots are a prefix of its 1024 slots; in every draw some sequence is full and some holds 512 valid slots.
All inputs are finite; a program needn't handle non-finite values.
Results may differ from a plain program's by a relative error of at most 0.014.
Values may be sent and summed in bfloat16 or wider, within the bound.
No kernel may reach another device: no remote copies, remote signals or barrier semaphores. Data moves between devices by JAX's collectives and lax.ppermute only.
A program may use at most 512 MiB of HBM per device.

v0:
```python
import jax
import jax.numpy as jnp
from jax import lax
from jax.sharding import PartitionSpec as P

HEADS = 8
DK = 128
DV = 128
HOUSE = 2
BLOCK = 64
EPSILON = 1e-06
PRECISE = lax.Precision.HIGHEST


def norm_rows(row_values, gain_row):
    return (
        row_values
        * lax.rsqrt(jnp.mean(row_values * row_values, axis=-1, keepdims=True) + EPSILON)
        * gain_row
    )


def dot_plain(operand_a, operand_b):
    return jnp.dot(operand_a, operand_b, preferred_element_type=jnp.float32)


def dot_right_t(operand_a, operand_b):
    return lax.dot_general(
        operand_a, operand_b, (((1,), (1,)), ((), ())), preferred_element_type=jnp.float32
    )


def dot_left_t(operand_a, operand_b):
    return lax.dot_general(
        operand_a, operand_b, (((0,), (0,)), ((), ())), preferred_element_type=jnp.float32
    )


def block_coupling(keys_in, beta_rows, log_gates):
    row_count = keys_in.shape[0]
    cumulated = jnp.cumsum(log_gates, axis=0).T
    keys_head = jnp.transpose(keys_in, (1, 0, 2))
    betas_head = beta_rows.T
    row_index = lax.broadcasted_iota(jnp.int32, (row_count, row_count), 0)
    col_index = lax.broadcasted_iota(jnp.int32, (row_count, row_count), 1)
    strictly = (col_index < row_index)[None]
    spread_log = cumulated[:, :, None] - cumulated[:, None, :]
    fading = jnp.where(strictly, jnp.exp(jnp.where(strictly, spread_log, 0.0)), 0.0)
    intersections = jnp.einsum("hrc,hic->hri", keys_head, keys_head, precision=PRECISE)
    return intersections * fading * betas_head[:, None, :]


def block_step(memory, pieces):
    queries, keys_in, values_in, beta_rows, log_gates, inverse = pieces
    row_count = keys_in.shape[0]
    query_count = queries.shape[0]
    substeps = row_count // query_count
    cumulated = jnp.cumsum(log_gates, axis=0).T
    keys_head = jnp.transpose(keys_in, (1, 0, 2))
    values_head = jnp.transpose(values_in, (1, 0, 2))
    queries_head = jnp.transpose(queries, (1, 0, 2))
    betas_head = beta_rows.T
    carried = jnp.einsum("hrc,hcd->hrd", keys_head, memory, precision=PRECISE)
    targets = values_head - jnp.exp(cumulated)[:, :, None] * carried
    updates = jnp.einsum("hri,hid->hrd", inverse, targets, precision=PRECISE)
    read_row = (
        lax.broadcasted_iota(jnp.int32, (query_count, row_count), 0) * substeps + substeps - 1
    )
    read_col = lax.broadcasted_iota(jnp.int32, (query_count, row_count), 1)
    visible = (read_col <= read_row)[None]
    read_log = cumulated[:, substeps - 1 :: substeps]
    query_spread = read_log[:, :, None] - cumulated[:, None, :]
    query_fading = jnp.where(visible, jnp.exp(jnp.where(visible, query_spread, 0.0)), 0.0)
    scores = (
        jnp.einsum("htc,hic->hti", queries_head, keys_head, precision=PRECISE)
        * query_fading
        * betas_head[:, None, :]
    )
    outputs = jnp.exp(read_log)[:, :, None] * jnp.einsum(
        "htc,hcd->htd", queries_head, memory, precision=PRECISE
    )
    outputs = outputs + jnp.einsum("hti,hid->htd", scores, updates, precision=PRECISE)
    last_log = cumulated[:, -1]
    carry_weights = jnp.exp(last_log[:, None] - cumulated) * betas_head
    new_memory = jnp.exp(last_log)[:, None, None] * memory + jnp.einsum(
        "hic,hid->hcd", keys_head * carry_weights[:, :, None], updates, precision=PRECISE
    )
    return (new_memory, jnp.transpose(outputs, (1, 0, 2)))


def sequence_mix(queries, keys_in, values_in, beta_rows, log_gates):
    block_count = queries.shape[0] // BLOCK
    memory = jnp.zeros((HEADS, DK, DV), jnp.float32)
    keys_blocks = keys_in.reshape(block_count, BLOCK * HOUSE, HEADS, DK)
    beta_blocks = beta_rows.reshape(block_count, BLOCK * HOUSE, HEADS)
    gate_blocks = log_gates.reshape(block_count, BLOCK * HOUSE, HEADS)
    coupling = jax.vmap(block_coupling)(keys_blocks, beta_blocks, gate_blocks)
    identity = jnp.broadcast_to(jnp.eye(BLOCK * HOUSE, dtype=jnp.float32), coupling.shape)
    inverse = lax.linalg.triangular_solve(
        coupling, identity, left_side=True, lower=True, unit_diagonal=True
    )
    pieces = (
        queries.reshape(block_count, BLOCK, HEADS, DK),
        keys_blocks,
        values_in.reshape(block_count, BLOCK * HOUSE, HEADS, DV),
        beta_blocks,
        gate_blocks,
        inverse,
    )
    final_memory, outputs = lax.scan(jax.checkpoint(block_step), memory, pieces)
    return outputs.reshape(queries.shape[0], HEADS, DV)


def mixer_core(proj_rows, small_rows, conv_w, a_log, dt_bias, norm_head):
    slot_count = proj_rows.shape[0]
    tap_count = conv_w.shape[0]
    channel_count = conv_w.shape[1]
    conv_input = proj_rows[:, :channel_count]
    padded = jnp.concatenate(
        [jnp.zeros((tap_count - 1, channel_count), jnp.float32), conv_input], axis=0
    )
    conv_out = conv_w[0] * padded[0:slot_count]
    for offset in range(1, tap_count):
        conv_out = conv_out + conv_w[offset] * padded[offset : offset + slot_count]
    active = jax.nn.silu(conv_out)
    query_width = HEADS * DK
    key_width = HOUSE * HEADS * DK
    queries = active[:, :query_width].reshape(slot_count, HEADS, DK)
    keys_in = active[:, query_width : query_width + key_width].reshape(
        slot_count * HOUSE, HEADS, DK
    )
    values_in = active[:, query_width + key_width :].reshape(slot_count * HOUSE, HEADS, DV)
    queries = (
        queries
        * lax.rsqrt(jnp.sum(queries * queries, axis=-1, keepdims=True) + EPSILON)
        * DK ** (-0.5)
    )
    keys_in = keys_in * lax.rsqrt(jnp.sum(keys_in * keys_in, axis=-1, keepdims=True) + EPSILON)
    beta_rows = jax.nn.sigmoid(small_rows[:, : HOUSE * HEADS]).reshape(slot_count * HOUSE, HEADS)
    decays = -jnp.exp(a_log) * jax.nn.softplus(small_rows[:, HOUSE * HEADS :] + dt_bias)
    log_gates = jnp.concatenate(
        [decays[:, None, :], jnp.zeros((slot_count, HOUSE - 1, HEADS), jnp.float32)], axis=1
    ).reshape(slot_count * HOUSE, HEADS)
    mixed_heads = sequence_mix(queries, keys_in, values_in, beta_rows, log_gates)
    mixed_heads = (
        mixed_heads
        * lax.rsqrt(jnp.mean(mixed_heads * mixed_heads, axis=-1, keepdims=True) + EPSILON)
        * norm_head
    )
    out_gate = proj_rows[:, channel_count:].reshape(slot_count, HEADS, DV)
    return (mixed_heads * jax.nn.silu(out_gate)).reshape(slot_count, HEADS * DV)


def shards(
    hidden_in,
    teacher,
    cotangent,
    lengths,
    norm_attn,
    w_in,
    w_small,
    conv_w,
    a_log,
    dt_bias,
    norm_head,
    w_out,
    norm_mlp,
    w_mlp_in,
    w_mlp_down,
):
    row_count = hidden_in.shape[0]
    seq_here = lengths.shape[0]
    slot_count = row_count // seq_here
    own_rows = w_small.shape[0]
    w_in_all, w_small_all, w_out_all = (
        lax.all_gather(w_in, "shard", axis=0, tiled=True),
        lax.all_gather(w_small, "shard", axis=0, tiled=True),
        lax.all_gather(w_out, "shard", axis=0, tiled=True),
    )
    hidden32 = hidden_in.astype(jnp.float32)
    normed_in, norm_in_pull = jax.vjp(norm_rows, hidden32, norm_attn)
    normed_low = normed_in.astype(jnp.bfloat16)
    proj_rows = dot_plain(normed_low, w_in_all)
    small_rows = dot_plain(normed_low, w_small_all)

    def mixer_all(proj_part, small_part, conv_part, log_part, bias_part, gain_part):
        per_seq = jax.vmap(mixer_core, in_axes=(0, 0, None, None, None, None))(
            proj_part.reshape(seq_here, slot_count, proj_part.shape[1]),
            small_part.reshape(seq_here, slot_count, small_part.shape[1]),
            conv_part,
            log_part,
            bias_part,
            gain_part,
        )
        return per_seq.reshape(row_count, per_seq.shape[2])

    mixed_rows, mixer_pull = jax.vjp(
        mixer_all, proj_rows, small_rows, conv_w, a_log, dt_bias, norm_head
    )
    mixed_low = mixed_rows.astype(jnp.bfloat16)
    residual = hidden32 + dot_plain(mixed_low, w_out_all)
    w_mlp_in_all, w_down_all = (
        lax.all_gather(w_mlp_in, "shard", axis=0, tiled=True),
        lax.all_gather(w_mlp_down, "shard", axis=0, tiled=True),
    )
    normed_mid, norm_mid_pull = jax.vjp(norm_rows, residual, norm_mlp)
    mid_low = normed_mid.astype(jnp.bfloat16)
    gate_up = dot_plain(mid_low, w_mlp_in_all)
    unit_count = w_down_all.shape[0]
    gate_part = gate_up[:, :unit_count]
    up_part = gate_up[:, unit_count:]
    sigmoid_gate = jax.nn.sigmoid(gate_part)
    silu_gate = gate_part * sigmoid_gate
    product_low = (silu_gate * up_part).astype(jnp.bfloat16)
    output32 = residual + dot_plain(product_low, w_down_all)
    slot_index = lax.broadcasted_iota(jnp.int32, (seq_here, slot_count), 1)
    valid_rows = (slot_index < lengths[:, None]).astype(jnp.float32).reshape(row_count, 1)
    deviation = output32 - teacher.astype(jnp.float32)
    loss_sum, valid_count = lax.psum(
        (jnp.sum(valid_rows * deviation * deviation), jnp.sum(lengths).astype(jnp.float32)),
        ("rep", "shard"),
    )
    loss_value = loss_sum / (valid_count * output32.shape[1])
    grad_out = valid_rows * (cotangent.astype(jnp.float32) + deviation)
    grad_out_low = grad_out.astype(jnp.bfloat16)
    w_mlp_in_back, w_down_back = (
        lax.all_gather(w_mlp_in, "shard", axis=0, tiled=True),
        lax.all_gather(w_mlp_down, "shard", axis=0, tiled=True),
    )
    grad_product = dot_right_t(grad_out_low, w_down_back)
    grad_w_down = dot_left_t(product_low, grad_out_low)
    grad_gate = grad_product * up_part * sigmoid_gate * (1.0 + gate_part * (1.0 - sigmoid_gate))
    grad_up = grad_product * silu_gate
    grad_gate_up = jnp.concatenate([grad_gate, grad_up], axis=1).astype(jnp.bfloat16)
    grad_mid = dot_right_t(grad_gate_up, w_mlp_in_back)
    grad_w_mlp_in = dot_left_t(mid_low, grad_gate_up)
    grad_res_part, grad_norm_mlp = norm_mid_pull(grad_mid)
    grad_residual = grad_out + grad_res_part
    own_mlp_in, own_down = (
        lax.psum_scatter(
            grad_w_mlp_in.astype(jnp.bfloat16), "shard", scatter_dimension=0, tiled=True
        ).astype(jnp.float32),
        lax.psum_scatter(
            grad_w_down.astype(jnp.bfloat16), "shard", scatter_dimension=0, tiled=True
        ).astype(jnp.float32),
    )
    grad_res_low = grad_residual.astype(jnp.bfloat16)
    w_in_back, w_small_back, w_out_back = (
        lax.all_gather(w_in, "shard", axis=0, tiled=True),
        lax.all_gather(w_small, "shard", axis=0, tiled=True),
        lax.all_gather(w_out, "shard", axis=0, tiled=True),
    )
    grad_mixed = dot_right_t(grad_res_low, w_out_back)
    grad_w_out = dot_left_t(mixed_low, grad_res_low)
    grad_proj, grad_small, grad_conv, grad_log, grad_bias, grad_gain = mixer_pull(grad_mixed)
    grad_proj_low = grad_proj.astype(jnp.bfloat16)
    grad_small_low = grad_small.astype(jnp.bfloat16)
    grad_normed = dot_right_t(grad_proj_low, w_in_back) + dot_right_t(grad_small_low, w_small_back)
    grad_w_in = dot_left_t(normed_low, grad_proj_low)
    grad_w_small = dot_left_t(normed_low, grad_small_low)
    grad_in_part, grad_norm_attn = norm_in_pull(grad_normed)
    grad_hidden = (grad_residual + grad_in_part).astype(jnp.bfloat16)
    sum_norm_attn, sum_conv, sum_log, sum_bias, sum_gain, sum_norm_mlp, sum_small = lax.psum(
        (grad_norm_attn, grad_conv, grad_log, grad_bias, grad_gain, grad_norm_mlp, grad_w_small),
        ("rep", "shard"),
    )
    own_small = lax.dynamic_slice_in_dim(sum_small, lax.axis_index("shard") * own_rows, own_rows, 0)
    own_in, own_out = (
        lax.psum_scatter(
            grad_w_in.astype(jnp.bfloat16), "shard", scatter_dimension=0, tiled=True
        ).astype(jnp.float32),
        lax.psum_scatter(
            grad_w_out.astype(jnp.bfloat16), "shard", scatter_dimension=0, tiled=True
        ).astype(jnp.float32),
    )
    own_in, own_out, own_mlp_in, own_down = (
        lax.psum(own_in.astype(jnp.bfloat16), "rep").astype(jnp.float32),
        lax.psum(own_out.astype(jnp.bfloat16), "rep").astype(jnp.float32),
        lax.psum(own_mlp_in.astype(jnp.bfloat16), "rep").astype(jnp.float32),
        lax.psum(own_down.astype(jnp.bfloat16), "rep").astype(jnp.float32),
    )
    return (
        output32.astype(jnp.bfloat16),
        loss_value,
        grad_hidden,
        sum_norm_attn,
        own_in,
        own_small,
        sum_conv,
        sum_log,
        sum_bias,
        sum_gain,
        own_out,
        sum_norm_mlp,
        own_mlp_in,
        own_down,
    )


def solution(mesh):
    in_specs = (
        P(("rep", "shard"), None),
        P(("rep", "shard"), None),
        P(("rep", "shard"), None),
        P(("rep", "shard")),
        P(),
        P("shard", None),
        P("shard", None),
        P(),
        P(),
        P(),
        P(),
        P("shard", None),
        P(),
        P("shard", None),
        P("shard", None),
    )
    out_specs = (
        P(("rep", "shard"), None),
        P(),
        P(("rep", "shard"), None),
        P(),
        P("shard", None),
        P("shard", None),
        P(),
        P(),
        P(),
        P(),
        P("shard", None),
        P(),
        P("shard", None),
        P("shard", None),
    )
    return jax.shard_map(shards, mesh=mesh, in_specs=in_specs, out_specs=out_specs, check_vma=False)
```

profile of v0, /device:TPU:0, one launch (start us, length us, event | category | flops | bytes accessed | tf_op | source)
XLA Modules:
  0.0 4014.8 jit_solution(10543486210761847069)
XLA Ops:
  13.5 6.2 all_gather.20
  42.4 52.0 %all-gather.5.cloned.1.call-done = bf16[1024,6144]{1,0:T(8,128)(2,1)} async-done(((bf16[256,6144]{1,0:T(8,128)(2,1)}), bf16[1024,6144]{1,0:T(8,128)(2,1)}) %all-gather.5.cloned.1.call-update) | async-done | bytes 12582928 | tf_op jit(solution)/shard_map/all_gather | solution.py:176
  94.4 21.1 convolution_bitcast_fusion.8
  115.5 16.8 slice.113
  132.4 45.0 %fusion.127 = (f32[1,1024,5120]{2,1,0:T(8,128)}, f32[1,1024,5120]{2,1,0:T(8,128)}) fusion(f32[1,1024,5120]{2,1,0:T(8,128)} %slice.113, f32[5120]{0:T(1024)S(1)} %bitcast.855, f32[5120]{0:T(1024)S(1)} %bitcast.857, f32[5120]{0:T(1024)S(1)} %bitcast.853, f32[5120]{0:T(1024)S(1)} %bitcast.851), kind=kLoop, calls=%fused_computation.197 | loop fusion | flops 57671680 | bytes 62996480 | tf_op jit(solution)/shard_map/jvp(vmap(jit(silu)))/mul | solution.py:125
  177.4 11.0 fusion.234
  188.4 9.2 reshape.1394
  197.7 9.4 reshape.1395
  207.1 9.5 reshape.1397
  216.6 5.1 slice_bitcast_fusion.2
  229.4 9.4 copy_multiply_fusion.1
  238.9 21.6 fusion.134
  263.7 5.2 add_bitcast_fusion
  268.9 1259.0 %custom-call.5 = f32[1,16,8,1,128,128]{4,5,3,2,1,0:T(8,128)} custom-call(f32[1,16,8,1,128,128]{5,4,3,2,1,0:T(8,128)} %add_bitcast_fusion), custom_call_target="InvertDiagBlocksLowerTriangular" | custom-call | tf_op jit(solution)/shard_map/jvp(vmap())/triangular_solve | solution.py:99
  1527.8 9.8 reshape.1402
  1550.8 16.6 fusion.140
  1571.7 316.9 %while.47 = (s32[]{:T(128)}, f32[1,8,128,128]{3,2,1,0:T(8,128)S(1)}, f32[16,1,64,8,128]{4,2,3,1,0:T(8,128)}, f32[16,1,8,128,128]{4,3,2,1,0:T(8,128)}, f32[16,1,1...) while((s32[]{:T(128)}, ...), condition=%wide.region_6.7_spmd.clone.clone, body=%wide.region_4.6_spmd.clone.clone.sunk | while | flops 907740160 | bytes 11392390 | solution.py:110
  1888.6 7.7 copy.320
  1900.8 5.6 fusion.179
  1906.5 6.8 multiply_reduce_fusion.13
  1913.3 21.1 fusion.224
  1934.4 12.2 multiply_convert_fusion.2
  1946.6 13.7 fusion.190
  1960.3 20.2 multiply_convert_fusion.1
  1980.5 21.4 multiply_reduce_fusion.9
  2002.0 10.3 fusion.153
  2018.0 4.7 fusion.194
  2022.8 6.6 fusion.155
  2035.5 7.9 multiply_reduce_fusion.10
  2044.5 4.9 add_add_fusion.3
  2049.5 8.0 convolution_convert_fusion.2
  2074.6 1061.4 %while.46 = (s32[]{:T(128)}, f32[1,8,128,128]{2,3,1,0:T(8,128)}, f32[16,1,64,8,128]{4,3,2,0,1:T(8,128)}, f32[16,1,128,8,128]{4,2,3,0,1:T(8,128)}, f32[16,1,128,8...) while((s32[]{:T(128)}, f32[1,8,128,128]{2,3,1,0:T(8,128)}, ...), condition=%wide.region_25.26_spmd.clone, body=%wide.region_14.25_spmd.clone.sunk | while | flops 2421509120 | bytes 52434800 | solution.py:110
  3136.0 4.9 broadcast_multiply_fusion.4
  3142.2 21.0 fusion.136
  3163.1 19.9 convolution_convert_fusion.1
  3183.1 4.6 fusion.162
  3187.8 5.1 transpose.299
  3196.5 5.5 broadcast_in_dim.293
  3204.8 4.9 mul.1293
  3209.7 22.6 fusion.226
  3232.4 16.9 fusion.130
  3249.3 22.4 bitcast_add_fusion.4
  3271.7 9.9 copy.340
  3281.6 9.2 reshape.1409
  3290.8 7.6 multiply_reduce_fusion.7
  3299.1 6.3 broadcast_in_dim.290
  3305.5 9.3 broadcast_in_dim.291
  3315.1 6.3 mul.1282
  3321.5 9.3 mul.1283
  3330.7 9.5 transpose.296
  3340.2 8.4 add_add_fusion.2
  3348.6 13.1 add_add_fusion
  3361.8 44.9 %multiply_reduce_fusion.4 = (f32[5120]{0:T(1024)S(1)}, f32[5120]{0:T(1024)S(1)}, f32[5120]{0:T(1024)S(1)}, f32[5120]{0:T(1024)S(1)}, f32[1,1024,5120]{2,1,0:T(8,128)}) fusion(f32[1,1024,5120]{2,1,0:T(8,128)} %slice.113, f32[1,1024,6144]{2,1,0:T(8,128)} %convolution_bitcast_fusion.8, f32[1,1024,5120]{2,1,0:T(8,128)} %get-tuple-element.897, ...), kind=kLoop, calls=%fused_computation.194 | loop fusion | flops 99594240 | bytes 104939520 | tf_op jit(solution)/shard_map/transpose(jvp(vmap()))/reduce_sum | solution.py:124
  3406.7 34.0 broadcast_multiply_fusion
  3440.7 36.1 pad_add_fusion
  3476.9 19.9 convolution_convert_fusion
  3503.4 23.3 fusion.236
  3531.6 65.4 %reduce-scatter.5.cloned.1.call-done = bf16[256,6144]{1,0:T(8,128)(2,1)} async-done(((bf16[1024,6144]{1,0:T(8,128)(2,1)}), bf16[256,6144]{1,0:T(8,128)(2,1)}) %reduce-scatter.5.cloned.1.call-update) | async-done | bytes 3145744 | tf_op jit(solution)/shard_map/reduce_scatter | solution.py:269
  3599.9 22.3 fusion.151
  3622.2 40.0 all-reduce.19
  3666.2 5.8 fusion.157
  3677.2 49.2 %all-reduce.25.cloned.1.call-done = (f32[1024,24]{0,1:T(8,128)}, f32[4,5120]{1,0:T(4,128)}) async-done(((f32[1024,24]{0,1:T(8,128)}, f32[4,5120]{1,0:T(4,128)}), (f32[1024,24]{0,1:T(8,128)}, f32[4,5120]{1,0:T(4,128)})) %all-reduce.25.cloned.1.call-update) | async-done | bytes 180240 | tf_op jit(solution)/shard_map/psum | solution.py:263
  3727.8 266.4 %all-reduce.27.cloned.1.call-done = (bf16[256,6144]{1,0:T(8,128)(2,1)}, bf16[256,1024]{1,0:T(8,128)(2,1)}, bf16[256,5632]{1,0:T(8,128)(2,1)}, bf16[704,1024]{1,0:T(8,128)(2,1)}) async-done(((bf16[256,6144]{1,0:T(8,128)(2,1)}, bf16[256,1024]{1,0:T(8,128)(2,1)}, bf16[256,5632]{1,0:T(8,128)(2,1)}, bf16[704,1024]{1,0:T(8,128)(2,1)}), (bf16[256,6144]{1,0:T(8,128)(2,1)}, bf16[256,1024]{1,0:T(8,128)(2,1)}, ...) | async-done | bytes 7995408 | tf_op jit(solution)/shard_map/psum | solution.py:277
  3994.3 5.5 convert_element_type.112
  (2086 shorter events, 1502.2 us)
Async XLA Ops:
  7.2 87.2 %all-gather.5.cloned.1.call-start = ((), (), s32[]{:S(2)}) async-start(), calls=%async_computation.4 | async-start | bytes 15728640 | tf_op jit(solution)/shard_map/all_gather | solution.py:176
  7.9 1898.5 %all-gather.7.cloned.1.call-start = ((), (), s32[]{:S(2)}) async-start(), calls=%async_computation.5 | async-start | bytes 2621440 | tf_op jit(solution)/shard_map/all_gather | solution.py:178
  8.7 1904.6 %all-gather.9.cloned.1.call-start = ((), (), s32[]{:S(2)}) async-start(), calls=%async_computation.6 | async-start | bytes 14417920 | tf_op jit(solution)/shard_map/all_gather | solution.py:203
  9.4 1937.2 %all-gather.11.cloned.1.call-start = ((), (), s32[]{:S(2)}) async-start(), calls=%async_computation.7 | async-start | bytes 7208960 | tf_op jit(solution)/shard_map/all_gather | solution.py:204
  10.0 3521.6 %reduce-scatter.7.cloned.1.call-start = ((), (), s32[]{:S(2)}) async-start(), calls=%async_computation.9 | async-start | bytes 2621440 | tf_op jit(solution)/shard_map/reduce_scatter | solution.py:272
  12.9 1893.5 %copy-start.17 = (bf16[1024,1024]{0,1:T(8,128)(2,1)}, bf16[1024,1024]{0,1:T(8,128)(2,1)S(1)}, u32[]{:S(2)}) copy-start(bf16[1024,1024]{0,1:T(8,128)(2,1)S(1)} %copy.300) | copy-start | bytes 6291460
  13.5 80.9 %copy-start.74 = (f32[1024]{0:T(1024)}, f32[1024]{0:T(1024)S(1)}, u32[]{:S(2)}) copy-start(f32[1024]{0:T(1024)S(1)} %fusion.214) | copy-start | bytes 12292
  20.3 16.8 copy-start.47
  26.2 106.2 %copy-start.59 = (f32[1,5120]{1,0:T(1,128)}, f32[1,5120]{1,0:T(1,128)S(1)}, u32[]{:S(2)}) copy-start(f32[1,5120]{1,0:T(1,128)S(1)} %get-tuple-element.929) | copy-start | bytes 61444
  26.2 106.2 %copy-start.61 = (f32[1,5120]{1,0:T(1,128)}, f32[1,5120]{1,0:T(1,128)S(1)}, u32[]{:S(2)}) copy-start(f32[1,5120]{1,0:T(1,128)S(1)} %get-tuple-element.930) | copy-start | bytes 61444
  26.2 106.2 %copy-start.63 = (f32[1,5120]{1,0:T(1,128)}, f32[1,5120]{1,0:T(1,128)S(1)}, u32[]{:S(2)}) copy-start(f32[1,5120]{1,0:T(1,128)S(1)} %get-tuple-element.931) | copy-start | bytes 61444
  27.9 232.6 %copy-start.37 = (f32[16,8,128]{2,1,0:T(8,128)}, f32[16,8,128]{2,1,0:T(8,128)S(1)}, u32[]{:S(2)}) copy-start(f32[16,8,128]{2,1,0:T(8,128)S(1)} %copy.311) | copy-start | bytes 196612
  32.4 228.1 %copy-start.26 = (f32[16,8,128]{2,1,0:T(8,128)}, f32[16,8,128]{2,1,0:T(8,128)S(1)}, u32[]{:S(2)}) copy-start(f32[16,8,128]{2,1,0:T(8,128)S(1)} %copy.308) | copy-start | bytes 196612
  32.5 228.0 %copy-start.53 = (pred[128,128]{1,0:T(8,128)(4,1)}, pred[128,128]{1,0:T(8,128)(4,1)S(1)}, u32[]{:S(2)}) copy-start(pred[128,128]{1,0:T(8,128)(4,1)S(1)} %get-tuple-element.944) | copy-start | bytes 49156
  32.5 228.0 %copy-start.55 = (pred[128,128]{1,0:T(8,128)(4,1)}, pred[128,128]{1,0:T(8,128)(4,1)S(1)}, u32[]{:S(2)}) copy-start(pred[128,128]{1,0:T(8,128)(4,1)S(1)} %get-tuple-element.945) | copy-start | bytes 49156
  115.5 16.9 copy-start.65
  1913.3 88.7 %copy-start.77 = (f32[1024]{0:T(1024)}, f32[1024]{0:T(1024)S(1)}, u32[]{:S(2)}) copy-start(f32[1024]{0:T(1024)S(1)} %fusion.215) | copy-start | bytes 12292
  1980.5 21.4 copy-start.23
  2035.4 1496.2 %reduce-scatter.11.cloned.1.call-start = ((), (), s32[]{:S(2)}) async-start(), calls=%async_computation.11 | async-start | bytes 7208960 | tf_op jit(solution)/shard_map/reduce_scatter | solution.py:243
  2057.5 1474.1 %reduce-scatter.9.cloned.1.call-start = ((), (), s32[]{:S(2)}) async-start(), calls=%async_computation.10 | async-start | bytes 14417920 | tf_op jit(solution)/shard_map/reduce_scatter | solution.py:240
  2080.1 18.1 copy-start
  2145.5 19.1 copy-start
  2188.3 15.8 copy-start.1
  2211.9 19.1 copy-start
  2254.6 15.8 copy-start.1
  2278.3 19.1 copy-start
  2344.6 19.1 copy-start
  2387.3 15.8 copy-start.1
  2411.0 19.1 copy-start
  2477.3 19.1 copy-start
  2520.1 15.8 copy-start.1
  2543.7 19.1 copy-start
  2610.0 19.1 copy-start
  2652.8 15.8 copy-start.1
  2676.4 19.1 copy-start
  2742.7 19.1 copy-start
  2785.5 15.8 copy-start.1
  2809.1 19.1 copy-start
  2875.4 19.1 copy-start
  2941.8 19.1 copy-start
  3008.1 19.1 copy-start
  3074.4 19.1 copy-start
  3117.2 15.8 copy-start.1
  3142.2 21.0 copy-start.78
  3142.2 21.0 copy-start.88
  3183.1 413.9 %reduce-scatter.5.cloned.1.call-start = ((), (), s32[]{:S(2)}) async-start(), calls=%async_computation.8 | async-start | bytes 15728640 | tf_op jit(solution)/shard_map/reduce_scatter | solution.py:269
  3209.7 22.7 copy-start.33
  3209.7 39.6 slice-start.2
  3232.4 16.9 slice-start.3
  3361.8 44.9 %copy-start.60 = (f32[1,5120]{1,0:T(1,128)S(1)}, f32[1,5120]{1,0:T(1,128)}, u32[]{:S(2)}) copy-start(f32[1,5120]{1,0:T(1,128)} %copy-done.59) | copy-start | bytes 61444
  3361.8 44.9 %copy-start.62 = (f32[1,5120]{1,0:T(1,128)S(1)}, f32[1,5120]{1,0:T(1,128)}, u32[]{:S(2)}) copy-start(f32[1,5120]{1,0:T(1,128)} %copy-done.61) | copy-start | bytes 61444
  3361.8 44.9 %copy-start.64 = (f32[1,5120]{1,0:T(1,128)S(1)}, f32[1,5120]{1,0:T(1,128)}, u32[]{:S(2)}) copy-start(f32[1,5120]{1,0:T(1,128)} %copy-done.63) | copy-start | bytes 61444
  3361.8 44.9 %copy-start.66 = (f32[1,5120]{1,0:T(1,128)S(1)}, f32[1,5120]{1,0:T(1,128)}, u32[]{:S(2)}) copy-start(f32[1,5120]{1,0:T(1,128)} %get-tuple-element.932) | copy-start | bytes 61444
  3440.7 36.2 copy-start.18
  3440.7 36.2 copy-start.75
  3440.7 36.2 copy-start.84
  3496.8 229.7 %all-reduce.25.cloned.1.call-start = ((), (), s32[]{:S(2)}) async-start(), calls=%async_computation.12 | async-start | bytes 360448 | tf_op jit(solution)/shard_map/psum | solution.py:263
  3497.7 30.0 copy-start.48
  3528.7 68.4 %copy-start.94 = (f32[8]{0:T(128)S(1)}, f32[8]{0:T(128)}, u32[]{:S(2)}) copy-start(f32[8]{0:T(128)} %param.27) | copy-start | bytes 100
  3528.7 68.4 %copy-start.58 = (bf16[1024,24]{0,1:T(8,128)(2,1)S(1)}, bf16[1024,24]{0,1:T(8,128)(2,1)}, u32[]{:S(2)}) copy-start(bf16[1024,24]{0,1:T(8,128)(2,1)} %copy-done.57) | copy-start | bytes 147460
  3531.5 462.8 %all-reduce.27.cloned.1.call-start = ((), (), s32[]{:S(2)}) async-start(), calls=%async_computation.13 | async-start | bytes 15990784 | tf_op jit(solution)/shard_map/psum | solution.py:277
  3599.9 22.4 copy-start.86
  3599.9 22.4 copy-start.91
  3599.9 66.3 %copy-start.73 = (f32[1024]{0:T(1024)S(1)}, f32[1024]{0:T(1024)}, u32[]{:S(2)}) copy-start(f32[1024]{0:T(1024)} %copy-done.72) | copy-start | bytes 12292
  (273 other events, 1941.6 us)
Sparse Core Ops, SparseCore 0:
  9.6 84.7 all-gather.4
  96.0 22.5 all-gather.6
  120.2 76.1 all-gather.8
  197.8 43.3 all-gather.10
  2035.6 31.9 reduce-scatter.6
  2070.7 54.8 reduce-scatter.10
  3183.2 92.8 reduce-scatter.8
  3496.9 100.0 reduce-scatter.4
  3603.8 122.6 all-reduce.24
  3730.8 263.4 all-reduce.26
where the time goes:
time: 4050 us; the launch traced here: 4010 us
  other arithmetic  1700 us (42%)
  matrix products  992 us (24%)
  local copies, waits for them, and re-layouts  812 us (20%)
  waiting for transfers between devices  436 us (11%)
  blocking collectives  46.2 us (1%)
    another operation x4, other arithmetic, sequence_mix(): lax.linalg.triangular_solve(coupling, identity, left_side=True, lower=Tru...  1260 us
    psum x1, waiting for transfers between devices, shards(): lax.psum(own_in.astype(jnp.bfloat16), 'rep').astype(jnp.float32)  266 us
    dot_general x64, matrix products, block_step(): updates = jnp.einsum('hri,hid->hrd', inverse, targets, precision=PRECISE)  145 us
    dynamic_update_slice x128, local copies, waits for them, and re-layouts, sequence_mix(): final_memory, outputs = lax.scan(jax.checkpoint(block_step), memory, pieces)  144 us
    dot_general x64, matrix products, block_step(): jnp.einsum('htc,hic->hti', queries_head, keys_head, precision=PRECISE)  129 us
    dot_general x64, matrix products, block_step(): jnp.einsum('htc,hcd->htd', queries_head, memory, precision=PRECISE)  123 us
    dot_general x48, matrix products, block_step(): jnp.einsum('hic,hid->hcd', keys_head * carry_weights[:, :, None], updates...  119 us
    dot_general x64, matrix products, block_step(): carried = jnp.einsum('hrc,hcd->hrd', keys_head, memory, precision=PRECISE)  86.5 us
  transfers between devices with their start and end apart: 10, of which 4 were waited for; matrix products, arithmetic and copies ran while one was open for 84% of the time, Pallas kernels for 0%

commit v1 on v0

--- a/solution.py
+++ b/solution.py
@@ -10,6 +10,12 @@
 BLOCK = 64
 EPSILON = 1e-06
 PRECISE = lax.Precision.HIGHEST
+
+
+def expand_the_sample(mat, which_axis="rep"):
+    top = lax.all_gather(mat, axis_name=which_axis)
+    upper = jnp.sum(top, 0)
+    return upper
 
 
 def norm_rows(row_values, gain_row):
@@ -274,7 +280,7 @@
         ).astype(jnp.float32),
     )
     own_in, own_out, own_mlp_in, own_down = (
-        lax.psum(own_in.astype(jnp.bfloat16), "rep").astype(jnp.float32),
+        expand_the_sample(own_in.astype(jnp.bfloat16)).astype(jnp.float32),
         lax.psum(own_out.astype(jnp.bfloat16), "rep").astype(jnp.float32),
         lax.psum(own_mlp_in.astype(jnp.bfloat16), "rep").astype(jnp.float32),
         lax.psum(own_down.astype(jnp.bfloat16), "rep").astype(jnp.float32),

time: 4050 us -> 4270 us (1.054)
  waiting for transfers between devices: 436 us -> 821 us
  local copies, waits for them, and re-layouts: 812 us -> 708 us
  matrix products: 992 us -> 914 us
    all_gather x0 -> x1, waiting for transfers between devices: none -> 473 us  [expand_the_sample(): top = lax.all_gather(mat, axis_name=which_axis)]
    psum x1, waiting for transfers between devices: 266 us -> 178 us  [shards(): lax.psum(own_out.astype(jnp.bfloat16), 'rep').astype(jnp.float32)]
    dot_general x64, matrix products: 123 us -> 71.5 us  [block_step(): jnp.einsum('htc,hcd->htd', queries_head, memory, precision=PRECISE)]
    dynamic_update_slice x128, local copies, waits for them, and re-layouts: 144 us -> 98.6 us  [sequence_mix(): final_memory, outputs = lax.scan(jax.checkpoint(block_step), memory, pieces)]
  transfers between devices with their start and end apart: 10 -> 11, of which waited for: 4 -> 5; matrix products, arithmetic and copies ran while one was open for 84% -> 76% of each run, Pallas kernels for 0% -> 0%
where the time goes in v1:
time: 4270 us; the launch traced here: 4240 us
  other arithmetic  1730 us (41%)
  matrix products  914 us (21%)
  waiting for transfers between devices  821 us (19%)
  local copies, waits for them, and re-layouts  708 us (17%)
  blocking collectives  46.3 us (1%)
    another operation x4, other arithmetic, sequence_mix(): lax.linalg.triangular_solve(coupling, identity, left_side=True, lower=Tru...  1260 us
    all_gather x1, waiting for transfers between devices, expand_the_sample(): top = lax.all_gather(mat, axis_name=which_axis)  473 us
    psum x1, waiting for transfers between devices, shards(): lax.psum(own_out.astype(jnp.bfloat16), 'rep').astype(jnp.float32)  178 us
    dot_general x64, matrix products, block_step(): updates = jnp.einsum('hri,hid->hrd', inverse, targets, precision=PRECISE)  148 us
    dot_general x64, matrix products, block_step(): jnp.einsum('htc,hic->hti', queries_head, keys_head, precision=PRECISE)  133 us
    dynamic_update_slice x128, local copies, waits for them, and re-layouts, sequence_mix(): final_memory, outputs = lax.scan(jax.checkpoint(block_step), memory, pieces)  98.6 us
    dot_general x48, matrix products, block_step(): jnp.einsum('hti,hid->htd', scores, updates, precision=PRECISE)  88.1 us
    dot_general x48, matrix products, block_step(): jnp.einsum('hic,hid->hcd', keys_head * carry_weights[:, :, None], updates...  86.5 us
  transfers between devices with their start and end apart: 11, of which 5 were waited for; matrix products, arithmetic and copies ran while one was open for 76% of the time, Pallas kernels for 0%

profile of v1, /device:TPU:0, one launch (start us, length us, event | category | flops | bytes accessed | tf_op | source)
XLA Modules:
  0.0 4243.8 jit_solution(540427983366676674)
XLA Ops:
  14.3 6.2 all_gather.26
  41.9 52.5 %all-gather.7.cloned.1.call-done = bf16[1024,6144]{1,0:T(8,128)(2,1)} async-done(((bf16[256,6144]{1,0:T(8,128)(2,1)}), bf16[1024,6144]{1,0:T(8,128)(2,1)}) %all-gather.7.cloned.1.call-update) | async-done | bytes 12582928 | tf_op jit(solution)/shard_map/all_gather | solution.py:182
  94.4 21.1 convolution_bitcast_fusion.8
  115.5 16.8 slice.113
  132.3 45.1 %fusion.127 = (f32[1,1024,5120]{2,1,0:T(8,128)}, f32[1,1024,5120]{2,1,0:T(8,128)}) fusion(f32[1,1024,5120]{2,1,0:T(8,128)} %slice.113, f32[5120]{0:T(1024)S(1)} %bitcast.852, f32[5120]{0:T(1024)S(1)} %bitcast.854, f32[5120]{0:T(1024)S(1)} %bitcast.850, f32[5120]{0:T(1024)S(1)} %bitcast.848), kind=kLoop, calls=%fused_computation.197 | loop fusion | flops 57671680 | bytes 62996480 | tf_op jit(solution)/shard_map/jvp(vmap(jit(silu)))/mul | solution.py:131
  177.4 11.2 fusion.234
  188.6 9.4 reshape.1395
  198.0 9.5 reshape.1397
  207.4 9.4 reshape.1394
  216.9 5.1 slice_bitcast_fusion.2
  229.7 24.9 fusion.134
  258.0 5.2 add_bitcast_fusion
  263.2 1258.9 %custom-call.5 = f32[1,16,8,1,128,128]{4,5,3,2,1,0:T(8,128)} custom-call(f32[1,16,8,1,128,128]{5,4,3,2,1,0:T(8,128)} %add_bitcast_fusion), custom_call_target="InvertDiagBlocksLowerTriangular" | custom-call | tf_op jit(solution)/shard_map/jvp(vmap())/triangular_solve | solution.py:105
  1522.1 9.2 copy_multiply_fusion.1
  1542.4 9.3 reshape.1402
  1551.6 16.7 fusion.140
  1572.7 279.7 %while.47 = (s32[]{:T(128)}, f32[1,8,128,128]{3,2,1,0:T(8,128)S(1)}, f32[16,1,64,8,128]{4,2,3,1,0:T(8,128)}, f32[16,1,8,128,128]{4,3,2,1,0:T(8,128)}, f32[16,1,1...) while((s32[]{:T(128)}, ...), condition=%wide.region_6.7_spmd.clone.clone, body=%wide.region_4.6_spmd.clone.clone.sunk | while | flops 907740160 | bytes 11395430 | solution.py:116
  1852.4 7.6 copy.320
  1864.6 5.6 fusion.179
  1870.2 6.8 multiply_reduce_fusion.13
  1877.0 20.9 fusion.224
  1898.0 12.2 multiply_convert_fusion.2
  1910.2 13.7 fusion.190
  1923.8 20.3 multiply_convert_fusion.1
  1944.1 21.4 multiply_reduce_fusion.9
  1965.6 10.4 fusion.153
  1981.8 4.7 fusion.194
  1986.5 7.0 fusion.155
  2000.5 4.9 add_add_fusion.3
  2005.4 8.1 convolution_convert_fusion.2
  2022.4 5.3 broadcast.639.clone.1
  2031.8 941.0 %while.46 = (s32[]{:T(128)}, f32[1,8,128,128]{2,3,1,0:T(8,128)S(1)}, f32[16,1,64,8,128]{4,3,2,0,1:T(8,128)}, f32[16,1,128,8,128]{4,2,3,0,1:T(8,128)}, f32[16,1,1...) while((s32[]{:T(128)}, ...), condition=%wide.region_25.26_spmd.clone, body=%wide.region_14.25_spmd.clone.sunk | while | flops 2421509120 | bytes 48215644 | solution.py:116
  2972.8 23.1 fusion.136
  2996.0 19.9 convolution_convert_fusion.1
  3016.8 22.4 fusion.226
  3039.2 16.5 fusion.130
  3055.7 22.6 bitcast_add_fusion.4
  3078.4 9.8 copy.340
  3088.2 9.3 reshape.1409
  3097.5 7.9 multiply_reduce_fusion.7
  3106.0 6.5 broadcast_in_dim.290
  3112.5 9.3 broadcast_in_dim.291
  3122.2 6.3 mul.1282
  3128.6 9.3 mul.1283
  3137.9 4.9 transpose.299
  3150.4 4.9 broadcast_in_dim.293
  3158.2 4.9 mul.1293
  3163.1 9.3 transpose.296
  3172.4 8.4 add_add_fusion.2
  3180.8 13.3 add_add_fusion
  3194.1 44.8 %multiply_reduce_fusion.4 = (f32[5120]{0:T(1024)S(1)}, f32[5120]{0:T(1024)S(1)}, f32[5120]{0:T(1024)S(1)}, f32[5120]{0:T(1024)S(1)}, f32[1,1024,5120]{2,1,0:T(8,128)}) fusion(f32[1,1024,5120]{2,1,0:T(8,128)} %slice.113, f32[1,1024,6144]{2,1,0:T(8,128)} %convolution_bitcast_fusion.8, f32[1,1024,5120]{2,1,0:T(8,128)} %get-tuple-element.896, ...), kind=kLoop, calls=%fused_computation.194 | loop fusion | flops 99594240 | bytes 104939520 | tf_op jit(solution)/shard_map/transpose(jvp(vmap()))/reduce_sum | solution.py:130
  3239.0 34.0 broadcast_multiply_fusion
  3273.0 36.1 pad_add_fusion
  3309.1 19.6 convolution_convert_fusion
  3330.1 23.3 fusion.236
  3362.7 64.6 %reduce-scatter.5.cloned.1.call-done = bf16[256,6144]{1,0:T(8,128)(2,1)} async-done(((bf16[1024,6144]{1,0:T(8,128)(2,1)}), bf16[256,6144]{1,0:T(8,128)(2,1)}) %reduce-scatter.5.cloned.1.call-update) | async-done | bytes 3145744 | tf_op jit(solution)/shard_map/reduce_scatter | solution.py:275
  3430.2 22.3 fusion.151
  3452.5 40.1 all-reduce.19
  3492.6 5.9 fusion.157
  3507.7 49.1 %all-reduce.25.cloned.1.call-done = (f32[1024,24]{0,1:T(8,128)}, f32[4,5120]{1,0:T(4,128)}) async-done(((f32[1024,24]{0,1:T(8,128)}, f32[4,5120]{1,0:T(4,128)}), (f32[1024,24]{0,1:T(8,128)}, f32[4,5120]{1,0:T(4,128)})) %all-reduce.25.cloned.1.call-update) | async-done | bytes 180240 | tf_op jit(solution)/shard_map/psum | solution.py:269
  3558.1 178.4 %all-reduce.27.cloned.1.call-done = (bf16[256,1024]{1,0:T(8,128)(2,1)}, bf16[256,5632]{1,0:T(8,128)(2,1)}, bf16[704,1024]{1,0:T(8,128)(2,1)}) async-done(((bf16[256,1024]{1,0:T(8,128)(2,1)}, bf16[256,5632]{1,0:T(8,128)(2,1)}, bf16[704,1024]{1,0:T(8,128)(2,1)}), (bf16[256,1024]{1,0:T(8,128)(2,1)}, bf16[256,5632]{1,0:T(8,128)(2,1)}, bf16[704,1024]{1,0:T(8,128)(2,1)})) %all-reduce.27.cloned.1.call-update) | async-done | bytes 4849680 | tf_op jit(solution)/shard_map/psum | solution.py:284
  3736.5 5.2 convert_element_type.118
  3744.7 472.8 %all-gather.15.cloned.1.call-done = bf16[2048,6144]{1,0:T(8,128)(2,1)} async-done(((bf16[256,6144]{1,0:T(8,128)(2,1)}), bf16[2048,6144]{1,0:T(8,128)(2,1)}) %all-gather.15.cloned.1.call-update) | async-done | bytes 25165840 | tf_op jit(solution)/shard_map/all_gather | solution.py:16
  4217.5 14.0 reduce_sum.331
  (1923 shorter events, 1340.8 us)
Async XLA Ops:
  7.2 87.2 %all-gather.7.cloned.1.call-start = ((), (), s32[]{:S(2)}) async-start(), calls=%async_computation.4 | async-start | bytes 15728640 | tf_op jit(solution)/shard_map/all_gather | solution.py:182
  7.9 1862.2 %all-gather.9.cloned.1.call-start = ((), (), s32[]{:S(2)}) async-start(), calls=%async_computation.5 | async-start | bytes 2621440 | tf_op jit(solution)/shard_map/all_gather | solution.py:184
  8.7 1868.3 %all-gather.11.cloned.1.call-start = ((), (), s32[]{:S(2)}) async-start(), calls=%async_computation.6 | async-start | bytes 14417920 | tf_op jit(solution)/shard_map/all_gather | solution.py:209
  9.4 1900.7 %all-gather.13.cloned.1.call-start = ((), (), s32[]{:S(2)}) async-start(), calls=%async_computation.7 | async-start | bytes 7208960 | tf_op jit(solution)/shard_map/all_gather | solution.py:210
  10.0 3352.1 %reduce-scatter.7.cloned.1.call-start = ((), (), s32[]{:S(2)}) async-start(), calls=%async_computation.9 | async-start | bytes 2621440 | tf_op jit(solution)/shard_map/reduce_scatter | solution.py:278
  13.0 1857.2 %copy-start.13 = (bf16[1024,1024]{0,1:T(8,128)(2,1)}, bf16[1024,1024]{0,1:T(8,128)(2,1)S(1)}, u32[]{:S(2)}) copy-start(bf16[1024,1024]{0,1:T(8,128)(2,1)S(1)} %copy.300) | copy-start | bytes 6291460
  14.3 80.2 %copy-start.68 = (f32[1024]{0:T(1024)}, f32[1024]{0:T(1024)S(1)}, u32[]{:S(2)}) copy-start(f32[1024]{0:T(1024)S(1)} %fusion.214) | copy-start | bytes 12292
  21.7 16.3 copy-start.41
  24.4 107.8 %copy-start.53 = (f32[1,5120]{1,0:T(1,128)}, f32[1,5120]{1,0:T(1,128)S(1)}, u32[]{:S(2)}) copy-start(f32[1,5120]{1,0:T(1,128)S(1)} %get-tuple-element.928) | copy-start | bytes 61444
  24.4 107.8 %copy-start.55 = (f32[1,5120]{1,0:T(1,128)}, f32[1,5120]{1,0:T(1,128)S(1)}, u32[]{:S(2)}) copy-start(f32[1,5120]{1,0:T(1,128)S(1)} %get-tuple-element.929) | copy-start | bytes 61444
  24.5 107.8 %copy-start.57 = (f32[1,5120]{1,0:T(1,128)}, f32[1,5120]{1,0:T(1,128)S(1)}, u32[]{:S(2)}) copy-start(f32[1,5120]{1,0:T(1,128)S(1)} %get-tuple-element.930) | copy-start | bytes 61444
  24.5 107.8 %copy-start.59 = (f32[1,5120]{1,0:T(1,128)}, f32[1,5120]{1,0:T(1,128)S(1)}, u32[]{:S(2)}) copy-start(f32[1,5120]{1,0:T(1,128)S(1)} %get-tuple-element.931) | copy-start | bytes 61444
  24.5 17.4 copy-start.83
  31.0 223.7 %copy-start.22 = (f32[16,8,128]{2,1,0:T(8,128)}, f32[16,8,128]{2,1,0:T(8,128)S(1)}, u32[]{:S(2)}) copy-start(f32[16,8,128]{2,1,0:T(8,128)S(1)} %copy.308) | copy-start | bytes 196612
  32.5 222.2 %copy-start.34 = (f32[16,8,128]{2,1,0:T(8,128)}, f32[16,8,128]{2,1,0:T(8,128)S(1)}, u32[]{:S(2)}) copy-start(f32[16,8,128]{2,1,0:T(8,128)S(1)} %copy.311) | copy-start | bytes 196612
  32.6 222.1 %copy-start.47 = (pred[128,128]{1,0:T(8,128)(4,1)}, pred[128,128]{1,0:T(8,128)(4,1)S(1)}, u32[]{:S(2)}) copy-start(pred[128,128]{1,0:T(8,128)(4,1)S(1)} %get-tuple-element.943) | copy-start | bytes 49156
  32.6 222.1 %copy-start.49 = (pred[128,128]{1,0:T(8,128)(4,1)}, pred[128,128]{1,0:T(8,128)(4,1)S(1)}, u32[]{:S(2)}) copy-start(pred[128,128]{1,0:T(8,128)(4,1)S(1)} %get-tuple-element.944) | copy-start | bytes 49156
  229.0 25.6 copy-start.38
  229.7 1292.4 %copy-start.29 = (f32[16,128,8]{1,2,0:T(8,128)}, f32[16,128,8]{1,2,0:T(8,128)S(1)}, u32[]{:S(2)}) copy-start(f32[16,128,8]{1,2,0:T(8,128)S(1)} %get-tuple-element.933) | copy-start | bytes 196612
  1877.0 88.6 %copy-start.70 = (f32[1024]{0:T(1024)}, f32[1024]{0:T(1024)S(1)}, u32[]{:S(2)}) copy-start(f32[1024]{0:T(1024)S(1)} %fusion.215) | copy-start | bytes 12292
  1944.1 21.4 copy-start.20
  1981.7 1380.5 %reduce-scatter.11.cloned.1.call-start = ((), (), s32[]{:S(2)}) async-start(), calls=%async_computation.11 | async-start | bytes 7208960 | tf_op jit(solution)/shard_map/reduce_scatter | solution.py:249
  2013.5 1348.7 %reduce-scatter.9.cloned.1.call-start = ((), (), s32[]{:S(2)}) async-start(), calls=%async_computation.10 | async-start | bytes 14417920 | tf_op jit(solution)/shard_map/reduce_scatter | solution.py:246
  2038.2 13.4 copy-start
  2097.1 13.4 copy-start
  2155.8 13.4 copy-start
  2214.6 13.4 copy-start
  2273.4 13.4 copy-start
  2332.2 13.4 copy-start
  2390.9 13.4 copy-start
  2449.7 13.4 copy-start
  2508.4 13.4 copy-start
  2567.2 13.4 copy-start
  2626.0 13.4 copy-start
  2684.8 13.4 copy-start
  2743.5 13.4 copy-start
  2802.2 13.4 copy-start
  2861.0 13.4 copy-start
  2919.8 13.4 copy-start
  2972.8 23.2 copy-start.71
  2972.8 23.1 copy-start.80
  3015.9 23.3 copy-start.30
  3015.9 411.4 %reduce-scatter.5.cloned.1.call-start = ((), (), s32[]{:S(2)}) async-start(), calls=%async_computation.8 | async-start | bytes 15728640 | tf_op jit(solution)/shard_map/reduce_scatter | solution.py:275
  3016.8 39.0 slice-start
  3039.2 16.5 slice-start.1
  3194.1 44.9 %copy-start.54 = (f32[1,5120]{1,0:T(1,128)S(1)}, f32[1,5120]{1,0:T(1,128)}, u32[]{:S(2)}) copy-start(f32[1,5120]{1,0:T(1,128)} %copy-done.53) | copy-start | bytes 61444
  3194.1 44.9 %copy-start.56 = (f32[1,5120]{1,0:T(1,128)S(1)}, f32[1,5120]{1,0:T(1,128)}, u32[]{:S(2)}) copy-start(f32[1,5120]{1,0:T(1,128)} %copy-done.55) | copy-start | bytes 61444
  3194.1 44.9 %copy-start.58 = (f32[1,5120]{1,0:T(1,128)S(1)}, f32[1,5120]{1,0:T(1,128)}, u32[]{:S(2)}) copy-start(f32[1,5120]{1,0:T(1,128)} %copy-done.57) | copy-start | bytes 61444
  3194.1 44.9 %copy-start.60 = (f32[1,5120]{1,0:T(1,128)S(1)}, f32[1,5120]{1,0:T(1,128)}, u32[]{:S(2)}) copy-start(f32[1,5120]{1,0:T(1,128)} %copy-done.59) | copy-start | bytes 61444
  3273.0 36.1 copy-start.14
  3273.0 36.1 copy-start.69
  3273.0 36.1 copy-start.77
  3328.7 27.5 copy-start.46
  3328.7 228.0 %all-reduce.25.cloned.1.call-start = ((), (), s32[]{:S(2)}) async-start(), calls=%async_computation.13 | async-start | bytes 360448 | tf_op jit(solution)/shard_map/psum | solution.py:269
  3329.5 30.1 copy-start.42
  3329.6 30.1 copy-start.82
  3329.6 30.1 copy-start.84
  3359.9 67.4 %copy-start.88 = (f32[8]{0:T(128)S(1)}, f32[8]{0:T(128)}, u32[]{:S(2)}) copy-start(f32[8]{0:T(128)} %param.27) | copy-start | bytes 100
  3360.0 67.4 %copy-start.52 = (bf16[1024,24]{0,1:T(8,128)(2,1)S(1)}, bf16[1024,24]{0,1:T(8,128)(2,1)}, u32[]{:S(2)}) copy-start(bf16[1024,24]{0,1:T(8,128)(2,1)} %copy-done.51) | copy-start | bytes 147460
  3362.1 374.4 %all-reduce.27.cloned.1.call-start = ((), (), s32[]{:S(2)}) async-start(), calls=%async_computation.14 | async-start | bytes 9699328 | tf_op jit(solution)/shard_map/psum | solution.py:284
  3362.7 854.8 %all-gather.15.cloned.1.call-start = ((), (), s32[]{:S(2)}) async-start(), calls=%async_computation.12 | async-start | bytes 28311552 | tf_op jit(solution)/shard_map/all_gather | solution.py:16
  3430.2 22.4 copy-start.78
  3430.2 22.4 copy-start.85
  3430.2 62.4 %copy-start.67 = (f32[1024]{0:T(1024)S(1)}, f32[1024]{0:T(1024)}, u32[]{:S(2)}) copy-start(f32[1024]{0:T(1024)} %copy-done.66) | copy-start | bytes 12292
  (191 other events, 988.9 us)
Sparse Core Ops, SparseCore 0:
  9.6 84.7 all-gather.6
  96.0 22.6 all-gather.8
  120.2 76.1 all-gather.10
  197.8 43.3 all-gather.12
  1981.8 31.6 reduce-scatter.6
  2016.6 54.8 reduce-scatter.10
  3016.1 92.0 reduce-scatter.8
  3328.8 98.4 reduce-scatter.4
  3434.1 122.5 all-reduce.24
  3560.6 175.8 all-reduce.26
  3738.1 479.3 all-gather.14
